TPU v7x, 32 devices: a whole 2x2x4 slice. The times are simulated.
32 devices in a mesh: branch: 2 (over x), tok: 16 (over z, y, core).
Axes of the slice: x: 2, y: 2, z: 4, core: 2. Of those that a mesh axis runs over, the one named last changes fastest.
Arguments:
- teacher_hidden: bfloat16 [2, 256, 4096], P('branch', 'tok'), may hold values from -400 to 400
- teacher_gain: float32 [2, 4096], P('branch'), may hold values from 0.5 to 1.5
- teacher_head: bfloat16 [2, 4096, 20480], P('branch', None, 'tok'), may hold values from -30 to 30
- student_hidden: bfloat16 [256, 4096], P('branch'), may hold values from -400 to 400
- student_gain: float32 [4096], replicated, may hold values from 0.5 to 1.5
- student_head: bfloat16 [4096, 20480], P('branch', 'tok'), may hold values from -30 to 30
- cluster_weights: int32 [256, 2], P(None, 'branch'), may hold values from 0 to 64, as said below
- token_ids: int32 [256], P('branch'), may hold values from 0 to 20479
Outputs:
- grad_head: float32 [4096, 20480], P('branch', 'tok')
- grad_hidden: float32 [256, 4096], P('branch', 'tok')
- grad_gain: float32 [4096], P('tok')
Inputs may be any that keep to these rules, and one draw needn't show every extreme that they name: `cluster_weights`: each token's 2 weights sum to 64.
All inputs are finite; a program needn't handle non-finite values.
Results may differ from a plain program's by a relative error of at most 0.0063.
Values may be sent and summed in bfloat16 or wider, within the bound.
No kernel may reach another device: no remote copies, remote signals or barrier semaphores. Data moves between devices by JAX's collectives and lax.ppermute only.
A program may use at most 128 MiB of HBM per device.

v0:
```python
import jax
import jax.numpy as jnp
from jax import lax
from jax.sharding import PartitionSpec as P

DEN = 64
eps = 1e-05
mix_label = 0.25
loss_scale = 64.0


def merged(value, axis, combine):
    everything = jax.tree.map(lambda part: lax.all_gather(part, axis), value)
    leading = jax.tree.map(lambda part: part[0], everything)

    def step(k, so_far):
        return combine(so_far, jax.tree.map(lambda part: part[k], everything))

    return lax.fori_loop(1, lax.axis_size(axis), step, leading)


def normalize(hidden, gain):
    values = hidden.astype(jnp.float32)
    inv_scale = lax.rsqrt(jnp.mean(values * values, axis=-1, keepdims=True) + eps)
    return ((values * inv_scale * gain).astype(jnp.bfloat16), inv_scale)


def combine_stats(first, second):
    top = jnp.maximum(first[0], second[0])
    return (top, first[1] * jnp.exp(first[0] - top) + second[1] * jnp.exp(second[0] - top))


def probabilities(logits):
    local_max = jnp.max(logits, axis=1)
    local_scaled = jnp.exp(logits - local_max[:, None])
    row_max, row_total = merged((local_max, jnp.sum(local_scaled, axis=1)), "tok", combine_stats)
    scaled = local_scaled * jnp.exp(local_max - row_max)[:, None]
    return scaled / row_total[:, None]


def per_device(
    teacher_hidden,
    teacher_gain,
    teacher_head,
    student_hidden,
    student_gain,
    student_head,
    cluster_weights,
    token_ids,
):
    rows_here = student_hidden.shape[0]
    width = student_hidden.shape[1]
    head_cols = teacher_head.shape[2]
    branch_gain = teacher_gain[0]
    branch_head = teacher_head[0]
    normed, unused_scale = normalize(
        lax.all_gather(teacher_hidden[0], "tok", axis=0, tiled=True), branch_gain
    )
    teacher_logits = jnp.dot(normed, branch_head, preferred_element_type=jnp.float32)
    weight = cluster_weights[:, 0].astype(jnp.float32) / DEN
    terms = probabilities(teacher_logits) * weight[:, None]
    mixed_all = lax.psum(terms, "branch")
    mixed = lax.dynamic_slice_in_dim(mixed_all, lax.axis_index("branch") * rows_here, rows_here, 0)
    student_normed, inv_scale = normalize(student_hidden, student_gain)
    student_logits = jnp.dot(
        student_normed,
        lax.all_gather(student_head, "branch", axis=0, tiled=True),
        preferred_element_type=jnp.float32,
    )
    student_probs = probabilities(student_logits)
    offset = lax.axis_index("tok") * head_cols
    onehot = (
        token_ids[:, None] == offset + jnp.arange(head_cols, dtype=jnp.int32)[None, :]
    ).astype(jnp.float32)
    targets = (1.0 - mix_label) * mixed + mix_label * onehot
    logit_grads = (loss_scale * (student_probs - targets)).astype(jnp.bfloat16)
    contract = (((1,), (1,)), ((), ()))
    partial_grads = lax.dot_general(
        logit_grads,
        lax.all_gather(student_head, "branch", axis=0, tiled=True),
        contract,
        preferred_element_type=jnp.float32,
    )
    normed_grads = lax.psum_scatter(partial_grads, "tok", scatter_dimension=1, tiled=True)
    slice_width = normed_grads.shape[1]
    col_start = lax.axis_index("tok") * slice_width
    hidden_cols = lax.dynamic_slice_in_dim(student_hidden, col_start, slice_width, 1).astype(
        jnp.float32
    )
    gain_cols = lax.dynamic_slice_in_dim(student_gain, col_start, slice_width, 0)
    grad_gain = lax.psum(jnp.sum(normed_grads * hidden_cols * inv_scale, axis=0), "branch")
    row_dots = lax.psum(jnp.sum(gain_cols[None, :] * normed_grads * hidden_cols, axis=1), "tok")
    grad_hidden = (
        inv_scale * gain_cols[None, :] * normed_grads
        - hidden_cols * inv_scale**3 * row_dots[:, None] / width
    )
    exchanged = lax.all_to_all(student_normed, "branch", split_axis=1, concat_axis=0, tiled=True)
    all_grads = lax.all_gather(logit_grads, "branch", axis=0, tiled=True)
    grad_head = lax.dot_general(
        exchanged, all_grads, (((0,), (0,)), ((), ())), preferred_element_type=jnp.float32
    )
    return (grad_head, grad_hidden, grad_gain)


def solution(mesh):
    in_specs = (
        P("branch", "tok", None),
        P("branch", None),
        P("branch", None, "tok"),
        P("branch", None),
        P(),
        P("branch", "tok"),
        P(None, "branch"),
        P("branch"),
    )
    out_specs = (P("branch", "tok"), P("branch", "tok"), P("tok"))
    return jax.shard_map(
        per_device, mesh=mesh, in_specs=in_specs, out_specs=out_specs, check_vma=False
    )
```

profile of v0, /device:TPU:0, one launch (start us, length us, event | category | flops | bytes accessed | tf_op | source)
XLA Modules:
  0.0 349.2 jit_solution(5427056235205396135)
XLA Ops:
  10.4 1.6 fusion.9
  12.0 42.4 %all-gather.14.cloned.1.call-done = bf16[1,256,4096]{2,1,0:T(8,128)(2,1)} async-done(((bf16[1,16,4096]{2,1,0:T(8,128)(2,1)}), bf16[1,256,4096]{2,1,0:T(8,128)(2,1)}) %all-gather.14.cloned.1.call-update) | async-done | bytes 2097168 | tf_op jit(solution)/shard_map/all_gather | solution.py:57
  54.4 2.2 fusion.4
  56.6 7.1 %fusion.22 = (f32[256]{0:T(256)S(1)}, f32[256,1280]{1,0:T(8,128)S(1)}) fusion(bf16[1,4096,1280]{2,1,0:T(8,128)(2,1)} %param.14, bf16[1,256,4096]{2,1,0:T(8,128)(2,1)S(1)} %copy-done, f32[4096]{0:T(1024)S(1)} %bitcast.78, f32[256]{0:T(256)S(1)} %add_rsqrt_fusion), kind=kOutput, calls=%fused_computation.50 | convolution fusion | flops 2688876288 | bytes 13912064 | tf_op jit(solution)/shard_map/dot_general | solution.py:59
  64.0 19.1 %all-gather.8 = f32[16,1,256]{2,1,0:T(1,128)S(1)} all-gather(f32[1,1,256]{2,1,0:T(1,128)S(1)} %bitcast.76), channel_id=6, replica_groups=mesh['branch'=2,'tok'=16] {'tok'}, dimensions={0}, use_global_device_ids=true | all-gather | bytes 17408 | tf_op jit(solution)/shard_map/all_gather | solution.py:13
  83.1 17.4 %all-gather.7 = f32[16,1,256]{2,1,0:T(1,128)S(1)} all-gather(f32[1,1,256]{2,1,0:T(1,128)S(1)} %bitcast.71), channel_id=5, replica_groups=mesh['branch'=2,'tok'=16] {'tok'}, dimensions={0}, use_global_device_ids=true | all-gather | bytes 17408 | tf_op jit(solution)/shard_map/all_gather | solution.py:13
  100.6 0.8 while.35
  101.4 1.4 divide_multiply_fusion
  102.9 81.2 %all-gather.12.cloned.1.call-done = bf16[4096,1280]{1,0:T(8,128)(2,1)} async-done(((bf16[2048,1280]{1,0:T(8,128)(2,1)}), bf16[4096,1280]{1,0:T(8,128)(2,1)}) %all-gather.12.cloned.1.call-update) | async-done | bytes 10485776 | tf_op jit(solution)/shard_map/all_gather | solution.py:67
  184.1 6.0 %fusion.23 = (f32[128]{0:T(128)S(1)}, f32[128,1280]{1,0:T(8,128)S(1)}) fusion(bf16[128,4096]{0,1:T(8,128)(2,1)} %fusion.9, bf16[4096,1280]{1,0:T(8,128)(2,1)} %all-gather.12.cloned.1.call-done), kind=kOutput, calls=%fused_computation.51 | convolution fusion | flops 1342340992 | bytes 12190208 | tf_op jit(solution)/shard_map/dot_general | solution.py:65
  190.4 21.3 %all-gather.6 = f32[16,1,128]{2,1,0:T(1,128)S(1)} all-gather(f32[1,1,128]{2,1,0:T(1,128)S(1)} %bitcast.77), channel_id=3, replica_groups=mesh['branch'=2,'tok'=16] {'tok'}, dimensions={0}, use_global_device_ids=true | all-gather | bytes 8704 | tf_op jit(solution)/shard_map/all_gather | solution.py:13
  211.7 17.4 %all-gather.5 = f32[16,1,128]{2,1,0:T(1,128)S(1)} all-gather(f32[1,1,128]{2,1,0:T(1,128)S(1)} %bitcast.74), channel_id=2, replica_groups=mesh['branch'=2,'tok'=16] {'tok'}, dimensions={0}, use_global_device_ids=true | all-gather | bytes 8704 | tf_op jit(solution)/shard_map/all_gather | solution.py:13
  229.8 3.1 all-reduce.2.cloned.1.call-done
  232.9 1.4 multiply_convert_fusion
  234.3 8.7 %fusion.25 = f32[128,4096]{1,0:T(8,128)} fusion(bf16[128,1280]{1,0:T(8,128)(2,1)S(1)} %multiply_convert_fusion, bf16[4096,1280]{1,0:T(8,128)(2,1)} %all-gather.12.cloned.1.call-done), kind=kOutput, calls=%fused_computation.53 | convolution fusion | flops 1342177280 | bytes 12910592 | tf_op jit(solution)/shard_map/dot_general | solution.py:78
  243.0 3.6 %all-to-all-start = ((bf16[128,2,2048]{0,2,1:T(8,128)(2,1)}), bf16[128,2,2048]{0,2,1:T(8,128)(2,1)S(1)}, u32[]{:S(2)}, u32[]{:S(2)}) async-start(bf16[128,2,2048]{0,2,1:T(8,128)(2,1)} %bitcast.4), calls=%async_computation | async-start | bytes 2097152 | tf_op jit(solution)/shard_map/all_to_all | solution.py:97
  246.7 13.6 %all-to-all-done = bf16[128,2,2048]{0,2,1:T(8,128)(2,1)S(1)} async-done(((bf16[128,2,2048]{0,2,1:T(8,128)(2,1)}), bf16[128,2,2048]{0,2,1:T(8,128)(2,1)S(1)}, u32[]{:S(2)}, u32[]{:S(2)}) %all-to-all-start) | async-done | bytes 1048608 | tf_op jit(solution)/shard_map/all_to_all | solution.py:97
  260.9 9.1 %all_gather.44 = bf16[256,1280]{1,0:T(8,128)(2,1)S(1)} all-gather(bf16[128,1280]{1,0:T(8,128)(2,1)S(1)} %multiply_convert_fusion), channel_id=1, replica_groups=mesh['branch'=2,'tok'=16] {'branch'}, dimensions={0}, use_global_device_ids=true | all-gather | bytes 983040 | tf_op jit(solution)/shard_map/all_gather | solution.py:98
  269.9 5.7 %fusion.24 = f32[2048,1280]{1,0:T(8,128)} fusion(bf16[256,2048]{1,0:T(8,128)(2,1)S(1)} %bitcast.63, bf16[256,1280]{1,0:T(8,128)(2,1)S(1)} %all_gather.44), kind=kOutput, calls=%fused_computation.52 | convolution fusion | flops 1342177280 | bytes 12189696 | tf_op jit(solution)/shard_map/dot_general | solution.py:99
  275.6 29.3 %reduce-scatter.2.cloned.1.call-done = f32[128,256]{1,0:T(8,128)} async-done(((f32[128,4096]{1,0:T(8,128)}), f32[128,256]{1,0:T(8,128)}) %reduce-scatter.2.cloned.1.call-update) | async-done | bytes 131088 | tf_op jit(solution)/shard_map/reduce_scatter | solution.py:84
  305.0 1.0 fusion.21
  306.0 29.5 %psum.22 = f32[128]{0:T(128)S(1)} all-reduce(f32[128]{0:T(128)S(1)} %get-tuple-element.274), channel_id=1, replica_groups=mesh['branch'=2,'tok'=16] {'tok'}, use_global_device_ids=true, to_apply=%region_13.0 | all-reduce | flops 128 | bytes 1024 | tf_op jit(solution)/shard_map/psum | solution.py:92
  335.5 5.5 %psum.23 = f32[256]{0:T(256)} all-reduce(f32[256]{0:T(256)S(1)} %get-tuple-element.273), channel_id=1, replica_groups=mesh['branch'=2,'tok'=16] {'branch'}, use_global_device_ids=true, to_apply=%region_15.0 | all-reduce | flops 256 | bytes 2048 | tf_op jit(solution)/shard_map/psum | solution.py:91
  341.0 1.7 fusion.18
  (84 shorter events, 6.0 us)
Async XLA Ops:
  7.2 47.2 %all-gather.14.cloned.1.call-start = ((), (), s32[]{:S(2)}) async-start(), calls=%async_computation.5 | async-start | bytes 2228224 | tf_op jit(solution)/shard_map/all_gather | solution.py:57
  7.9 1.2 copy-start.1
  7.9 176.2 %all-gather.12.cloned.1.call-start = ((), (), s32[]{:S(2)}) async-start(), calls=%async_computation.2 | async-start | bytes 15728640 | tf_op jit(solution)/shard_map/all_gather | solution.py:67
  8.7 1.7 copy-start.3
  8.7 1.7 copy-start.2
  8.7 224.2 %all-reduce.2.cloned.1.call-start = ((), (), s32[]{:S(2)}) async-start(), calls=%async_computation.3 | async-start | bytes 2621440 | tf_op jit(solution)/shard_map/psum | solution.py:62
  10.4 46.2 %copy-start.5 = (f32[1,4096]{1,0:T(1,128)S(1)}, f32[1,4096]{1,0:T(1,128)}, u32[]{:S(2)}) copy-start(f32[1,4096]{1,0:T(1,128)} %param.13) | copy-start | bytes 49156
  54.3 2.3 copy-start
  102.9 130.0 %copy-start.4 = (s32[128]{0:T(128)S(1)}, s32[128]{0:T(128)}, u32[]{:S(2)}) copy-start(s32[128]{0:T(128)} %param.19) | copy-start | bytes 1540
  102.9 202.1 %reduce-scatter.2.cloned.1.call-start = ((), (), s32[]{:S(2)}) async-start(), calls=%async_computation.4 | async-start | bytes 2228224 | tf_op jit(solution)/shard_map/reduce_scatter | solution.py:84
  243.0 17.3 %all-to-all-start = ((bf16[128,2,2048]{0,2,1:T(8,128)(2,1)}), bf16[128,2,2048]{0,2,1:T(8,128)(2,1)S(1)}, u32[]{:S(2)}, u32[]{:S(2)}) async-start(bf16[128,2,2048]{0,2,1:T(8,128)(2,1)} %bitcast.4), calls=%async_computation | async-start | bytes 2097152 | tf_op jit(solution)/shard_map/all_to_all | solution.py:97
Sparse Core Ops, SparseCore 0:
  10.1 44.1 all-gather.13
  55.9 128.1 all-gather.11
  187.0 45.8 all-reduce.1
  243.2 61.7 reduce-scatter.1
where the time goes:
time: 350 us; the launch traced here: 349 us
  waiting for transfers between devices  171 us (49%)
  blocking collectives  119 us (34%)
  matrix products  27.5 us (8%)
  between operations  13.9 us (4%)
  other arithmetic  11.2 us (3%)
  starting transfers between devices  3.75 us (1%)
    all_gather x1, waiting for transfers between devices, per_device(): lax.all_gather(student_head, 'branch', axis=0, tiled=True)  81.2 us
    all_gather x4, blocking collectives, merged(): everything = jax.tree.map(lambda part: lax.all_gather(part, axis), value)  75.3 us
    all_gather x1, waiting for transfers between devices, per_device(): lax.all_gather(teacher_hidden[0], 'tok', axis=0, tiled=True)  42.4 us
    psum x1, blocking collectives, per_device(): lax.psum(jnp.sum(gain_cols[None, :] * normed_grads * hidden_cols, axis=1)...  29.5 us
    reduce_scatter x1, waiting for transfers between devices, per_device(): lax.psum_scatter(partial_grads, 'tok', scatter_dimension=1, tiled=True)  29.3 us
    all_to_all x1, waiting for transfers between devices, per_device(): lax.all_to_all(student_normed, 'branch', split_axis=1, concat_axis=0, til...  13.6 us
    all_gather x1, blocking collectives, per_device(): all_grads = lax.all_gather(logit_grads, 'branch', axis=0, tiled=True)  9.09 us
    dot_general x1, matrix products, per_device(): lax.dot_general(logit_grads, lax.all_gather(student_head, 'branch', axis=...  8.73 us
  transfers between devices with their start and end apart: 5, of which 5 were waited for; matrix products, arithmetic and copies ran while one was open for 8% of the time, Pallas kernels for 0%

commit v1 on v0

--- a/solution.py
+++ b/solution.py
@@ -64,7 +64,10 @@
     student_normed, inv_scale = normalize(student_hidden, student_gain)
     student_logits = jnp.dot(
         student_normed,
-        lax.all_gather(student_head, "branch", axis=0, tiled=True),
+        jnp.concatenate(
+            lax.all_to_all(jnp.stack([student_head] * lax.axis_size("branch")), "branch", 0, 0),
+            axis=0,
+        ),
         preferred_element_type=jnp.float32,
     )
     student_probs = probabilities(student_logits)

time: 350 us -> 477 us (1.36)
  waiting for transfers between devices: 171 us -> 281 us
  other arithmetic: 11.2 us -> 21.1 us
  starting transfers between devices: 3.75 us -> 11.5 us
    all_to_all x0 -> x1, waiting for transfers between devices: none -> 192 us  [per_device(): lax.all_to_all(jnp.stack([student_head] * lax.axis_size('branch')), 'bran...]
    all_gather x1, waiting for transfers between devices: 81.2 us -> 0.02 us  [per_device(): lax.all_gather(student_head, 'branch', axis=0, tiled=True)]
    another operation x0 -> x1, other arithmetic: none -> 9.22 us  [per_device(): jnp.stack([student_head] * lax.axis_size('branch'))]
    all_to_all x0 -> x1, starting transfers between devices: none -> 7.73 us  [per_device(): lax.all_to_all(jnp.stack([student_head] * lax.axis_size('branch')), 'bran...]
  transfers between devices with their start and end apart: 5 -> 6, of which waited for: 5 -> 4; matrix products, arithmetic and copies ran while one was open for 8% -> 6% of each run, Pallas kernels for 0% -> 0%
where the time goes in v1:
time: 477 us
  waiting for transfers between devices  281 us (59%)
  blocking collectives  119 us (25%)
  matrix products  27.4 us (6%)
  other arithmetic  21.1 us (4%)
  between operations  13.9 us (3%)
  starting transfers between devices  11.5 us (2%)
    all_to_all x1, waiting for transfers between devices, per_device(): lax.all_to_all(jnp.stack([student_head] * lax.axis_size('branch')), 'bran...  192 us
    all_gather x4, blocking collectives, merged(): everything = jax.tree.map(lambda part: lax.all_gather(part, axis), value)  74.5 us
    all_gather x1, waiting for transfers between devices, per_device(): lax.all_gather(teacher_hidden[0], 'tok', axis=0, tiled=True)  45.7 us
    psum x1, blocking collectives, per_device(): lax.psum(jnp.sum(gain_cols[None, :] * normed_grads * hidden_cols, axis=1)...  29.5 us
    reduce_scatter x1, waiting for transfers between devices, per_device(): lax.psum_scatter(partial_grads, 'tok', scatter_dimension=1, tiled=True)  27.6 us
    all_to_all x1, waiting for transfers between devices, per_device(): lax.all_to_all(student_normed, 'branch', split_axis=1, concat_axis=0, til...  14.3 us
    all_gather x1, blocking collectives, per_device(): all_grads = lax.all_gather(logit_grads, 'branch', axis=0, tiled=True)  9.76 us
  transfers between devices with their start and end apart: 6, of which 4 were waited for; matrix products, arithmetic and copies ran while one was open for 6% of the time, Pallas kernels for 0%

profile of v1, /device:TPU:0, one launch (start us, length us, event | category | flops | bytes accessed | tf_op | source)
XLA Modules:
  0.0 476.7 jit_solution(6709986545892632611)
XLA Ops:
  8.6 45.7 %all-gather.14.cloned.1.call-done = bf16[1,256,4096]{2,1,0:T(8,128)(2,1)} async-done(((bf16[1,16,4096]{2,1,0:T(8,128)(2,1)}), bf16[1,256,4096]{2,1,0:T(8,128)(2,1)}) %all-gather.14.cloned.1.call-update) | async-done | bytes 2097168 | tf_op jit(solution)/shard_map/all_gather | solution.py:57
  54.4 2.2 fusion.4
  56.6 7.0 %fusion.22 = (f32[256]{0:T(256)S(1)}, f32[256,1280]{1,0:T(8,128)S(1)}) fusion(bf16[1,4096,1280]{2,1,0:T(8,128)(2,1)} %param.14, bf16[1,256,4096]{2,1,0:T(8,128)(2,1)S(1)} %copy-done, f32[4096]{0:T(1024)S(1)} %bitcast.81, f32[256]{0:T(256)S(1)} %add_rsqrt_fusion), kind=kOutput, calls=%fused_computation.51 | convolution fusion | flops 2688876288 | bytes 13912064 | tf_op jit(solution)/shard_map/dot_general | solution.py:59
  64.0 19.2 %all-gather.8 = f32[16,1,256]{2,1,0:T(1,128)S(1)} all-gather(f32[1,1,256]{2,1,0:T(1,128)S(1)} %bitcast.79), channel_id=6, replica_groups=mesh['branch'=2,'tok'=16] {'tok'}, dimensions={0}, use_global_device_ids=true | all-gather | bytes 17408 | tf_op jit(solution)/shard_map/all_gather | solution.py:13
  83.1 17.4 %all-gather.7 = f32[16,1,256]{2,1,0:T(1,128)S(1)} all-gather(f32[1,1,256]{2,1,0:T(1,128)S(1)} %bitcast.74), channel_id=5, replica_groups=mesh['branch'=2,'tok'=16] {'tok'}, dimensions={0}, use_global_device_ids=true | all-gather | bytes 17408 | tf_op jit(solution)/shard_map/all_gather | solution.py:13
  101.5 1.5 divide_multiply_fusion
  102.9 9.2 %pad_maximum_fusion = bf16[2,2048,1280]{2,1,0:T(8,128)(2,1)} fusion(bf16[1,2048,1280]{2,1,0:T(8,128)(2,1)} %bitcast.65), kind=kLoop, calls=%fused_computation.9 | loop fusion | flops 5242880 | bytes 15728640 | tf_op jit(solution)/shard_map/stack | solution.py:68
  112.2 7.7 %all-to-all-start.1 = ((bf16[2,2048,1280]{2,1,0:T(8,128)(2,1)}), bf16[2,2048,1280]{2,1,0:T(8,128)(2,1)}, u32[]{:S(2)}, u32[]{:S(2)}) async-start(bf16[2,2048,1280]{2,1,0:T(8,128)(2,1)} %pad_maximum_fusion), calls=%async_computation.1 | async-start | bytes 20971520 | tf_op jit(solution)/shard_map/all_to_all | solution.py:68
  122.4 1.5 fusion.9
  123.9 192.1 %all-to-all-done.1 = bf16[2,2048,1280]{2,1,0:T(8,128)(2,1)} async-done(((bf16[2,2048,1280]{2,1,0:T(8,128)(2,1)}), bf16[2,2048,1280]{2,1,0:T(8,128)(2,1)}, u32[]{:S(2)}, u32[]{:S(2)}) %all-to-all-start.1) | async-done | bytes 10485792 | tf_op jit(solution)/shard_map/all_to_all | solution.py:68
  316.0 6.0 %fusion.23 = (f32[128]{0:T(128)S(1)}, f32[128,1280]{1,0:T(8,128)S(1)}) fusion(bf16[128,4096]{0,1:T(8,128)(2,1)} %fusion.9, bf16[4096,1280]{1,0:T(8,128)(2,1)} %bitcast.8), kind=kOutput, calls=%fused_computation.52 | convolution fusion | flops 1342340992 | bytes 12190208 | tf_op jit(solution)/shard_map/dot_general | solution.py:65
  322.3 20.4 %all-gather.6 = f32[16,1,128]{2,1,0:T(1,128)S(1)} all-gather(f32[1,1,128]{2,1,0:T(1,128)S(1)} %bitcast.80), channel_id=3, replica_groups=mesh['branch'=2,'tok'=16] {'tok'}, dimensions={0}, use_global_device_ids=true | all-gather | bytes 8704 | tf_op jit(solution)/shard_map/all_gather | solution.py:13
  342.7 17.4 %all-gather.5 = f32[16,1,128]{2,1,0:T(1,128)S(1)} all-gather(f32[1,1,128]{2,1,0:T(1,128)S(1)} %bitcast.77), channel_id=2, replica_groups=mesh['branch'=2,'tok'=16] {'tok'}, dimensions={0}, use_global_device_ids=true | all-gather | bytes 8704 | tf_op jit(solution)/shard_map/all_gather | solution.py:13
  360.8 1.4 multiply_convert_fusion
  362.3 8.7 %fusion.25 = f32[128,4096]{1,0:T(8,128)} fusion(bf16[128,1280]{1,0:T(8,128)(2,1)S(1)} %multiply_convert_fusion, bf16[4096,1280]{1,0:T(8,128)(2,1)} %all-gather.12.cloned.1.call-done), kind=kOutput, calls=%fused_computation.54 | convolution fusion | flops 1342177280 | bytes 12910592 | tf_op jit(solution)/shard_map/dot_general | solution.py:81
  371.0 3.6 all-to-all-start
  374.7 14.3 %all-to-all-done = bf16[128,2,2048]{0,2,1:T(8,128)(2,1)S(1)} async-done(((bf16[128,2,2048]{0,2,1:T(8,128)(2,1)}), bf16[128,2,2048]{0,2,1:T(8,128)(2,1)S(1)}, u32[]{:S(2)}, u32[]{:S(2)}) %all-to-all-start) | async-done | bytes 1048608 | tf_op jit(solution)/shard_map/all_to_all | solution.py:100
  389.5 9.8 %all_gather.42 = bf16[256,1280]{1,0:T(8,128)(2,1)S(1)} all-gather(bf16[128,1280]{1,0:T(8,128)(2,1)S(1)} %multiply_convert_fusion), channel_id=1, replica_groups=mesh['branch'=2,'tok'=16] {'branch'}, dimensions={0}, use_global_device_ids=true | all-gather | bytes 983040 | tf_op jit(solution)/shard_map/all_gather | solution.py:101
  399.3 5.7 %fusion.24 = f32[2048,1280]{1,0:T(8,128)} fusion(bf16[256,2048]{1,0:T(8,128)(2,1)S(1)} %bitcast.66, bf16[256,1280]{1,0:T(8,128)(2,1)S(1)} %all_gather.42), kind=kOutput, calls=%fused_computation.53 | convolution fusion | flops 1342177280 | bytes 12189696 | tf_op jit(solution)/shard_map/dot_general | solution.py:102
  404.9 27.6 %reduce-scatter.2.cloned.1.call-done = f32[128,256]{1,0:T(8,128)} async-done(((f32[128,4096]{1,0:T(8,128)}), f32[128,256]{1,0:T(8,128)}) %reduce-scatter.2.cloned.1.call-update) | async-done | bytes 131088 | tf_op jit(solution)/shard_map/reduce_scatter | solution.py:87
  432.5 1.0 fusion.21
  433.6 29.5 %psum.22 = f32[128]{0:T(128)S(1)} all-reduce(f32[128]{0:T(128)S(1)} %get-tuple-element.274), channel_id=1, replica_groups=mesh['branch'=2,'tok'=16] {'tok'}, use_global_device_ids=true, to_apply=%region_13.0 | all-reduce | flops 128 | bytes 1024 | tf_op jit(solution)/shard_map/psum | solution.py:95
  463.1 5.5 %psum.23 = f32[256]{0:T(256)} all-reduce(f32[256]{0:T(256)S(1)} %get-tuple-element.273), channel_id=1, replica_groups=mesh['branch'=2,'tok'=16] {'branch'}, use_global_device_ids=true, to_apply=%region_15.0 | all-reduce | flops 256 | bytes 2048 | tf_op jit(solution)/shard_map/psum | solution.py:94
  468.5 1.7 fusion.18
  (85 shorter events, 7.6 us)
Async XLA Ops:
  7.2 49.4 %copy-start.4 = (f32[1,4096]{1,0:T(1,128)S(1)}, f32[1,4096]{1,0:T(1,128)}, u32[]{:S(2)}) copy-start(f32[1,4096]{1,0:T(1,128)} %param.13) | copy-start | bytes 49156
  7.2 47.2 %all-gather.14.cloned.1.call-start = ((), (), s32[]{:S(2)}) async-start(), calls=%async_computation.6 | async-start | bytes 2228224 | tf_op jit(solution)/shard_map/all_gather | solution.py:57
  7.9 352.9 %all-reduce.2.cloned.1.call-start = ((), (), s32[]{:S(2)}) async-start(), calls=%async_computation.3 | async-start | bytes 2621440 | tf_op jit(solution)/shard_map/psum | solution.py:62
  54.4 2.3 copy-start
  112.2 203.9 %all-to-all-start.1 = ((bf16[2,2048,1280]{2,1,0:T(8,128)(2,1)}), bf16[2,2048,1280]{2,1,0:T(8,128)(2,1)}, u32[]{:S(2)}, u32[]{:S(2)}) async-start(bf16[2,2048,1280]{2,1,0:T(8,128)(2,1)} %pad_maximum_fusion), calls=%async_computation.1 | async-start | bytes 20971520 | tf_op jit(solution)/shard_map/all_to_all | solution.py:68
  119.9 1.2 copy-start.1
  119.9 242.3 %all-gather.12.cloned.1.call-start = ((), (), s32[]{:S(2)}) async-start(), calls=%async_computation.4 | async-start | bytes 15728640 | tf_op jit(solution)/shard_map/all_gather | solution.py:83
  120.7 1.7 copy-start.2
  120.7 311.9 %reduce-scatter.2.cloned.1.call-start = ((), (), s32[]{:S(2)}) async-start(), calls=%async_computation.5 | async-start | bytes 2228224 | tf_op jit(solution)/shard_map/reduce_scatter | solution.py:87
  316.0 44.8 %copy-start.3 = (s32[128]{0:T(128)S(1)}, s32[128]{0:T(128)}, u32[]{:S(2)}) copy-start(s32[128]{0:T(128)} %param.19) | copy-start | bytes 1540
  371.0 18.0 %all-to-all-start = ((bf16[128,2,2048]{0,2,1:T(8,128)(2,1)}), bf16[128,2,2048]{0,2,1:T(8,128)(2,1)S(1)}, u32[]{:S(2)}, u32[]{:S(2)}) async-start(bf16[128,2,2048]{0,2,1:T(8,128)(2,1)} %bitcast.4), calls=%async_computation | async-start | bytes 2097152 | tf_op jit(solution)/shard_map/all_to_all | solution.py:100
Sparse Core Ops, SparseCore 0:
  10.1 44.1 all-gather.13
  103.1 61.9 all-reduce.1
  166.6 195.3 all-gather.11
  371.1 61.3 reduce-scatter.1
